TPU v7x, 256 devices: a whole 4x4x8 slice. The times are simulated.
256 devices in a mesh: row: 8 (over z_lo, x), col: 32 (over z_hi, y, core).
Axes of the slice: x: 4, y: 4, z: 8 (z_hi: 4, z_lo: 2; z = z_hi * 2 + z_lo), core: 2. Of those that a mesh axis runs over, the one named last changes fastest.
Arguments:
- wave_field: float32 [64, 128, 64, 128], P(None, 'col', 'row'), may hold values from -6 to 6
- medium_term: float32 [128, 64, 128], P('col', 'row'), may hold values from 0.5 to 4
- node_flux: float32 [64, 32, 8, 384], P(None, 'col', 'row'), may hold values from -6 to 6
- node_cell: int32 [32, 8, 384], P('col', 'row'), may hold values from 0 to 4095
- block_target: int32 [32, 8, 32], P('col', 'row'), may hold values from 0 to 31, as said below
- boundary_matrix: bfloat16 [2, 4096, 98304], P(None, 'row', 'col'), may hold values from -0.0390625 to 0.0390625
Outputs:
- volume_image: float32 [64, 128, 64, 128], P(None, 'col', 'row')
- boundary_image: float32 [4096, 64], P(('row', 'col'))
Inputs may be any that keep to these rules, and one draw needn't show every extreme that they name: For every brick (c, r), block_target[c, r, :] is a permutation of the 32 column blocks.
All inputs are finite; a program needn't handle non-finite values.
Results may differ from a plain program's by a relative error of at most 0.0029.
Values may be sent and summed in bfloat16 or wider, within the bound.
A program may use at most 64 MiB of HBM per device.

v0:
```python
import jax
import jax.numpy as jnp
from jax import lax
from jax.sharding import PartitionSpec as P


def in_order(tiles, dim):
    tiles = jnp.moveaxis(tiles, 0, dim)
    lengths = tiles.shape
    return tiles.reshape(*lengths[:dim], lengths[dim] * lengths[dim + 1], *lengths[dim + 2 :])


def sent_to_all(x, axis):
    count = lax.axis_size(axis)
    return lax.all_to_all(jnp.broadcast_to(x[None], (count, *x.shape)), axis, 0, 0, tiled=True)


def gather_directly(x, axis, dim):
    return in_order(sent_to_all(x, axis), dim)


def padded_2(block, sides, width):
    for axis, dim in sides:
        count = lax.axis_size(axis)
        forward = [(i, i + 1) for i in range(count - 1)]
        backward = [(target, source) for source, target in forward]
        low = lax.ppermute(
            lax.slice_in_dim(block, block.shape[dim] - width, None, axis=dim), axis, forward
        )
        high = lax.ppermute(lax.slice_in_dim(block, 0, width, axis=dim), axis, backward)
        block = jnp.concatenate([low, block, high], axis=dim)
    return block


def in_blocks(x, dim, count):
    lengths = x.shape
    tiles = x.reshape(*lengths[:dim], count, lengths[dim] // count, *lengths[dim + 1 :])
    return jnp.moveaxis(tiles, dim, 0)


def sum_at_owner(x, axis, dim):
    count = lax.axis_size(axis)
    tiles = lax.all_to_all(in_blocks(x, dim, count), axis, 0, 0, tiled=True)
    return jnp.sum(tiles, axis=0)


def three_tap(values, axis, side_weight, centre_weight):
    length = values.shape[axis]
    lower = lax.slice_in_dim(values, 0, length - 2, axis=axis)
    middle = lax.slice_in_dim(values, 1, length - 1, axis=axis)
    upper = lax.slice_in_dim(values, 2, length, axis=axis)
    return side_weight * (lower + upper) + centre_weight * middle


def on_device(wave_field, medium_term, node_flux, node_cell, block_target, boundary_matrix):
    components, width_x, width_y, depth_cells = wave_field.shape
    cell_total = width_x * width_y * depth_cells
    angles = components // 2
    col_count = lax.axis_size("col")
    node_total = node_cell.shape[-1]
    slot_len = node_total // col_count
    targets = block_target.reshape(col_count)
    block_ids = jnp.arange(col_count, dtype=jnp.int32)
    matches = targets[None, :] == block_ids[:, None]
    slot_cells = node_cell.reshape(col_count, slot_len)
    ordered = jnp.sum(jnp.where(matches[:, :, None], slot_cells[None, :, :], 0), axis=1).reshape(
        node_total
    )
    flat_field = wave_field.reshape(components, cell_total)
    traces = jnp.take(flat_field, ordered, axis=1).astype(jnp.bfloat16)
    received = lax.all_to_all(traces, "col", split_axis=1, concat_axis=1, tiled=True)
    column_traces = gather_directly(received, "row", 1)
    padded = padded_2(wave_field, (("row", 2), ("col", 1)), 1)
    padded = jnp.pad(padded, ((0, 0), (0, 0), (0, 0), (1, 1)))
    elem_z = three_tap(padded, 3, 1.0 / 6.0, 2.0 / 3.0)
    lapl_z = three_tap(padded, 3, -1.0, 2.0)
    lump_z = three_tap(padded, 3, 1.0 / 3.0, 2.0 / 3.0)
    elem_yz = three_tap(elem_z, 2, 1.0 / 6.0, 2.0 / 3.0)
    lapl_y_elem_z = three_tap(elem_z, 2, -1.0, 2.0)
    elem_y_lapl_z = three_tap(lapl_z, 2, 1.0 / 6.0, 2.0 / 3.0)
    lump_yz = three_tap(lump_z, 2, 1.0 / 3.0, 2.0 / 3.0)
    stiffness = three_tap(elem_yz, 1, -1.0, 2.0) + three_tap(
        lapl_y_elem_z + elem_y_lapl_z, 1, 1.0 / 6.0, 2.0 / 3.0
    )
    mass_sum = three_tap(lump_yz, 1, 1.0 / 3.0, 2.0 / 3.0)
    volume_image = stiffness - medium_term[None] * mass_sum
    flat_image = volume_image.reshape(components, cell_total)
    flat_image = flat_image.at[:, node_cell.reshape(node_total)].add(
        -node_flux.reshape(components, node_total)
    )
    volume_image = flat_image.reshape(components, width_x, width_y, depth_cells)
    slab_rows = boundary_matrix.shape[1]
    column_span = boundary_matrix.shape[2]
    own_rows = slab_rows // col_count
    products = lax.dot_general(
        boundary_matrix.reshape(2 * (own_rows * lax.axis_size("col")), column_span),
        column_traces,
        (((1,), (1,)), ((), ())),
        preferred_element_type=jnp.float32,
    )
    real_part = products[: own_rows * lax.axis_size("col")]
    imag_part = products[own_rows * lax.axis_size("col") :]
    boundary_image = sum_at_owner(
        jnp.concatenate(
            [
                real_part[:, :angles] - imag_part[:, angles:],
                imag_part[:, :angles] + real_part[:, angles:],
            ],
            axis=1,
        ),
        "col",
        0,
    )
    return (volume_image, boundary_image)


def solution(mesh):
    in_specs = (
        P(None, "col", "row", None),
        P("col", "row", None),
        P(None, "col", "row", None),
        P("col", "row", None),
        P("col", "row", None),
        P(None, "row", "col"),
    )
    out_specs = (P(None, "col", "row", None), P(("row", "col"), None))
    return jax.shard_map(
        on_device, mesh=mesh, in_specs=in_specs, out_specs=out_specs, check_vma=False
    )
```

profile of v0, /device:TPU:1, one launch (start us, length us, event | category | flops | bytes accessed | tf_op | source)
XLA Modules:
  0.0 84.1 jit_solution(6091311905287193799)
XLA Ops:
  0.6 0.0 copy-start
  0.7 2.1 %fusion.19 = (f32[64,4,1,128]{3,2,1,0:T(1,128)S(1)}, f32[64,4,1,128]{3,2,1,0:T(1,128)S(1)}) fusion(f32[64,4,8,128]{3,2,1,0:T(8,128)} %param.6), kind=kLoop, calls=%fused_computation.54 | loop fusion | bytes 524288 | tf_op jit(solution)/shard_map/slice | solution.py:28
  2.8 1.3 %collective-permute-start.1 = (f32[64,4,1,128]{3,0,2,1:T(8,128)S(1)}, f32[64,4,1,128]{3,0,2,1:T(8,128)S(1)}, u32[]{:S(2)}, u32[]{:S(2)}) collective-permute-start(f32[64,4,1,128]{3,0,2,1:T(8,128)S(1)} %copy.46), channel_id=1, source_target_pairs={{32,0},{64,32},{96,64},{128,96},{160,128},{192,160},{224,192},{33,... | collective-permute-start | bytes 393224 | tf_op jit(solution)/shard_map/ppermute | solution.py:30
  4.1 0.0 copy-start.2
  4.1 4.7 %collective-permute-start = (f32[64,4,1,128]{3,0,2,1:T(8,128)S(1)}, f32[64,4,1,128]{3,0,2,1:T(8,128)S(1)}, u32[]{:S(2)}, u32[]{:S(2)}) collective-permute-start(f32[64,4,1,128]{3,0,2,1:T(8,128)S(1)} %copy.45), channel_id=1, source_target_pairs={{0,32},{32,64},{64,96},{96,128},{128,160},{160,192},{192,224},{1,3... | collective-permute-start | bytes 393224 | tf_op jit(solution)/shard_map/ppermute | solution.py:27
  8.9 1.8 %copy.38 = bf16[64,4,8,128]{0,3,2,1:T(8,128)(2,1)S(1)} copy(f32[64,4,8,128]{3,2,1,0:T(8,128)} %param.6) | data formatting | bytes 1572864 | tf_op args[0]
  10.7 0.1 broadcast_in_dim.45
  10.8 0.1 copy.36
  10.9 0.3 select_reduce_fusion
  11.2 0.1 copy.39
  11.3 0.1 reshape.128
  11.4 1.4 %gather_fusion = bf16[384,64]{1,0:T(8,128)(2,1)S(1)} fusion(bf16[64,4096]{0,1:T(8,128)(2,1)S(1)} %bitcast.32, s32[1024]{0:T(1024)S(1)} %pad_clamp_fusion), kind=kCustom, calls=%fused_computation | custom fusion | bytes 99840 | tf_op jit(solution)/shard_map/jit(_take)/gather | solution.py:70
  12.9 0.1 copy.37
  13.0 0.0 collective-permute-done.1
  13.0 0.1 copy.33
  13.2 0.1 copy.32
  13.3 0.2 pad_maximum_fusion.3
  13.5 5.1 %collective-permute-start.3 = (f32[64,1,10,128]{3,2,1,0:T(8,128)S(1)}, f32[64,1,10,128]{3,2,1,0:T(8,128)S(1)}, u32[]{:S(2)}, u32[]{:S(2)}) collective-permute-start(f32[64,1,10,128]{3,2,1,0:T(8,128)S(1)} %get-tuple-element.16), channel_id=1, source_target_pairs={{1,0},{2,1},{3,2},{4,3},{5,4},{6,5},{7,6},{8,7},{9,8},{10,9},{11,1... | collective-permute-start | bytes 983048 | tf_op jit(solution)/shard_map/ppermute | solution.py:30
  18.6 1.9 %collective-permute-start.2 = (f32[64,1,10,128]{3,2,1,0:T(8,128)S(1)}, f32[64,1,10,128]{3,2,1,0:T(8,128)}, u32[]{:S(2)}, u32[]{:S(2)}) collective-permute-start(f32[64,1,10,128]{3,2,1,0:T(8,128)S(1)} %get-tuple-element.15), channel_id=1, source_target_pairs={{0,1},{1,2},{2,3},{3,4},{4,5},{5,6},{6,7},{7,8},{8,9},{9,10},{10,1... | collective-permute-start | bytes 983048 | tf_op jit(solution)/shard_map/ppermute | solution.py:27
  20.6 0.1 fusion.20
  20.7 0.8 reshape.153
  21.5 13.0 %all-to-all-start = ((bf16[32,2,384]{2,1,0:T(2,128)(2,1)}), bf16[32,2,384]{2,1,0:T(2,128)(2,1)S(1)}, u32[]{:S(2)}, u32[]{:S(2)}) async-start(bf16[32,2,384]{2,1,0:T(2,128)(2,1)} %reshape.153), calls=%async_computation | async-start | bytes 98304 | tf_op jit(solution)/shard_map/all_to_all | solution.py:71
  34.5 0.1 neg.6
  34.6 0.8 copy.47
  35.4 0.6 fusion.17
  36.0 8.6 %all-to-all-done = bf16[32,2,384]{2,1,0:T(2,128)(2,1)S(1)} async-done(((bf16[32,2,384]{2,1,0:T(2,128)(2,1)}), bf16[32,2,384]{2,1,0:T(2,128)(2,1)S(1)}, u32[]{:S(2)}, u32[]{:S(2)}) %all-to-all-start) | async-done | bytes 49184 | tf_op jit(solution)/shard_map/all_to_all | solution.py:71
  44.6 0.1 reshape.154
  44.8 0.1 copy.40
  44.9 0.8 broadcast_in_dim.51
  45.7 5.5 %all-to-all-start.1 = ((bf16[8,64,384]{2,1,0:T(8,128)(2,1)}), bf16[8,64,384]{2,1,0:T(8,128)(2,1)S(1)}, u32[]{:S(2)}, u32[]{:S(2)}) async-start(bf16[8,64,384]{2,1,0:T(8,128)(2,1)} %broadcast_in_dim.51), calls=%async_computation.1 | async-start | bytes 786432 | tf_op jit(solution)/shard_map/all_to_all | solution.py:15
  51.2 1.5 %pad_maximum_fusion = f32[64,6,10,128]{3,2,1,0:T(8,128)S(1)} fusion(f32[64,1,10,128]{3,2,1,0:T(8,128)S(1)} %collective-permute-done.3, f32[64,4,1,128]{3,2,1,0:T(1,128)S(1)} %copy.33, f32[64,4,8,128]{3,2,1,0:T(8,128)S(1)} %copy-done, f32[64,4,1,128]{3,2,1,0:T(1,128)S(1)} %copy.32, f32[64,1,10,128]{3,2,1,0:T(8,128)} %collective-permute-done.2), kind=kLoop, calls=%fused_computation.5 | loop fusion | flops 1966080 | bytes 3932160 | tf_op jit(solution)/shard_map/concatenate | solution.py:31
  52.7 5.0 %multiply_add_fusion.2 = (f32[64,6,10,128]{3,2,1,0:T(8,128)S(1)}, f32[64,6,10,128]{3,2,1,0:T(8,128)S(1)}, f32[64,6,10,128]{3,2,1,0:T(8,128)S(1)}) fusion(f32[64,6,10,128]{3,2,1,0:T(8,128)S(1)} %pad_maximum_fusion), kind=kLoop, calls=%fused_computation.8 | loop fusion | flops 5406720 | bytes 7864320 | tf_op jit(solution)/shard_map/add | solution.py:52
  57.7 1.6 %fusion.1 = f32[64,6,8,128]{3,2,1,0:T(8,128)} fusion(f32[64,6,10,128]{3,2,1,0:T(8,128)S(1)} %get-tuple-element.14), kind=kLoop, calls=%fused_computation.10 | loop fusion | flops 1572864 | bytes 6291456 | tf_op jit(solution)/shard_map/add | solution.py:52
  59.3 1.0 %multiply_add_fusion.3 = (f32[64,6,8,128]{3,2,1,0:T(8,128)S(1)}, f32[64,6,8,128]{3,2,1,0:T(8,128)S(1)}) fusion(f32[64,6,10,128]{3,2,1,0:T(8,128)S(1)} %get-tuple-element.12, f32[64,6,10,128]{3,2,1,0:T(8,128)S(1)} %get-tuple-element.13), kind=kLoop, calls=%fused_computation.19 | loop fusion | flops 4718592 | bytes 12582912 | tf_op jit(solution)/shard_map/add | solution.py:52
  60.4 0.0 copy-start.3
  60.4 4.8 %convolution_bitcast_fusion = f32[1024,64]{0,1:T(8,128)S(1)} fusion(bf16[64,3072]{1,0:T(8,128)(2,1)S(1)} %bitcast.34, bf16[1024,3072]{1,0:T(8,128)(2,1)} %bitcast.31), kind=kOutput, calls=%fused_computation.20 | convolution fusion | flops 402653184 | bytes 6946816 | tf_op jit(solution)/shard_map/dot_general | solution.py:95
  65.2 0.1 copy.42
  65.4 0.8 reshape.155
  66.2 4.2 %all-to-all-start.2 = ((f32[32,1,1024]{2,1,0:T(1,128)}), f32[32,1,1024]{2,1,0:T(1,128)S(1)}, u32[]{:S(2)}, u32[]{:S(2)}) async-start(f32[32,1,1024]{2,1,0:T(1,128)} %reshape.155), calls=%async_computation.2 | async-start | bytes 262144 | tf_op jit(solution)/shard_map/all_to_all | solution.py:43
  70.4 3.5 %fusion.8 = f32[64,4,8,128]{3,2,1,0:T(8,128)} fusion(f32[64,6,8,128]{3,2,1,0:T(8,128)} %fusion.1, f32[64,6,8,128]{3,2,1,0:T(8,128)S(1)} %get-tuple-element.11, f32[64,6,8,128]{3,2,1,0:T(8,128)S(1)} %get-tuple-element.10, f32[4,8,128]{2,1,0:T(8,128)S(1)} %copy-done.3), kind=kLoop, calls=%fused_computation.24 | loop fusion | flops 3932160 | bytes 10502144 | tf_op jit(solution)/shard_map/sub | solution.py:86
  73.9 1.9 %copy.34 = f32[64,4,8,128]{0,3,2,1:T(8,128)S(1)} copy(f32[64,4,8,128]{3,2,1,0:T(8,128)} %fusion.8) | data formatting | bytes 2097152 | tf_op jit(solution)/shard_map/sub | solution.py:86
  75.8 3.7 %scatter_custom_fusion = f32[64,4096]{0,1:T(8,128)S(1)} fusion(f32[64,4096]{0,1:T(8,128)S(1)} %bitcast.29, s32[384]{0:T(512)} %fusion.17, f32[64,1,1,384]{0,3,1,2:T(8,128)S(1)} %copy-done.1), kind=kCustom, calls=%fused_computation.40 | custom fusion | flops 24576 | bytes 1245184 | tf_op jit(solution)/shard_map/scatter-add | solution.py:88
  79.5 1.8 %copy.43 = f32[64,4,8,128]{3,2,1,0:T(8,128)} copy(f32[64,4,8,128]{0,3,2,1:T(8,128)S(1)} %bitcast.30) | data formatting | bytes 2097152
  81.3 0.6 all-to-all-done.2
  81.9 0.5 broadcast.88
  82.4 0.9 %reduce.5 = f32[32,1024]{1,0:T(8,128)S(1)} reduce(f32[32,1,1024]{2,1,0:T(1,128)S(1)} %all-to-all-done.2, f32[]{:T(128)} %broadcast.88), dimensions={1}, to_apply=%all_to_all.12.reduce_sub_computation | reduce | bytes 262148 | tf_op jit(solution)/shard_map/all_to_all | solution.py:43
  83.4 0.1 reshape.156
  83.5 0.6 reduce_sum.19
  (25 shorter events, 0.3 us)
Async XLA Ops:
  0.6 12.7 %copy-start = (f32[64,4,8,128]{3,2,1,0:T(8,128)S(1)}, f32[64,4,8,128]{3,2,1,0:T(8,128)}, u32[]{:S(2)}) copy-start(f32[64,4,8,128]{3,2,1,0:T(8,128)} %param.6) | copy-start | bytes 3145732
  0.6 10.0 %copy-start.4 = (s32[1,1,384]{2,1,0:T(1,128)S(1)}, s32[1,1,384]{2,1,0:T(1,128)}, u32[]{:S(2)}) copy-start(s32[1,1,384]{2,1,0:T(1,128)} %param.9) | copy-start | bytes 4612
  0.7 10.2 %copy-start.5 = (s32[1,1,32]{2,1,0:T(1,128)S(1)}, s32[1,1,32]{2,1,0:T(1,128)}, u32[]{:S(2)}) copy-start(s32[1,1,32]{2,1,0:T(1,128)} %param.10) | copy-start | bytes 388
  2.8 10.2 %collective-permute-start.1 = (f32[64,4,1,128]{3,0,2,1:T(8,128)S(1)}, f32[64,4,1,128]{3,0,2,1:T(8,128)S(1)}, u32[]{:S(2)}, u32[]{:S(2)}) collective-permute-start(f32[64,4,1,128]{3,0,2,1:T(8,128)S(1)} %copy.46), channel_id=1, source_target_pairs={{32,0},{64,32},{96,64},{128,96},{160,128},{192,160},{224,192},{33,... | collective-permute-start | bytes 393224 | tf_op jit(solution)/shard_map/ppermute | solution.py:30
  4.1 30.3 %copy-start.2 = (f32[64,1,1,384]{3,2,1,0:T(1,128)S(1)}, f32[64,1,1,384]{3,2,1,0:T(1,128)}, u32[]{:S(2)}) copy-start(f32[64,1,1,384]{3,2,1,0:T(1,128)} %param.8) | copy-start | bytes 294916
  4.1 9.0 %collective-permute-start = (f32[64,4,1,128]{3,0,2,1:T(8,128)S(1)}, f32[64,4,1,128]{3,0,2,1:T(8,128)S(1)}, u32[]{:S(2)}, u32[]{:S(2)}) collective-permute-start(f32[64,4,1,128]{3,0,2,1:T(8,128)S(1)} %copy.45), channel_id=1, source_target_pairs={{0,32},{32,64},{64,96},{96,128},{128,160},{160,192},{192,224},{1,3... | collective-permute-start | bytes 393224 | tf_op jit(solution)/shard_map/ppermute | solution.py:27
  13.5 37.6 %collective-permute-start.3 = (f32[64,1,10,128]{3,2,1,0:T(8,128)S(1)}, f32[64,1,10,128]{3,2,1,0:T(8,128)S(1)}, u32[]{:S(2)}, u32[]{:S(2)}) collective-permute-start(f32[64,1,10,128]{3,2,1,0:T(8,128)S(1)} %get-tuple-element.16), channel_id=1, source_target_pairs={{1,0},{2,1},{3,2},{4,3},{5,4},{6,5},{7,6},{8,7},{9,8},{10,9},{11,1... | collective-permute-start | bytes 983048 | tf_op jit(solution)/shard_map/ppermute | solution.py:30
  18.6 32.5 %collective-permute-start.2 = (f32[64,1,10,128]{3,2,1,0:T(8,128)S(1)}, f32[64,1,10,128]{3,2,1,0:T(8,128)}, u32[]{:S(2)}, u32[]{:S(2)}) collective-permute-start(f32[64,1,10,128]{3,2,1,0:T(8,128)S(1)} %get-tuple-element.15), channel_id=1, source_target_pairs={{0,1},{1,2},{2,3},{3,4},{4,5},{5,6},{6,7},{7,8},{8,9},{9,10},{10,1... | collective-permute-start | bytes 983048 | tf_op jit(solution)/shard_map/ppermute | solution.py:27
  21.5 23.2 %all-to-all-start = ((bf16[32,2,384]{2,1,0:T(2,128)(2,1)}), bf16[32,2,384]{2,1,0:T(2,128)(2,1)S(1)}, u32[]{:S(2)}, u32[]{:S(2)}) async-start(bf16[32,2,384]{2,1,0:T(2,128)(2,1)} %reshape.153), calls=%async_computation | async-start | bytes 98304 | tf_op jit(solution)/shard_map/all_to_all | solution.py:71
  45.7 14.6 %all-to-all-start.1 = ((bf16[8,64,384]{2,1,0:T(8,128)(2,1)}), bf16[8,64,384]{2,1,0:T(8,128)(2,1)S(1)}, u32[]{:S(2)}, u32[]{:S(2)}) async-start(bf16[8,64,384]{2,1,0:T(8,128)(2,1)} %broadcast_in_dim.51), calls=%async_computation.1 | async-start | bytes 786432 | tf_op jit(solution)/shard_map/all_to_all | solution.py:15
  60.4 10.0 %copy-start.3 = (f32[4,8,128]{2,1,0:T(8,128)S(1)}, f32[4,8,128]{2,1,0:T(8,128)}, u32[]{:S(2)}) copy-start(f32[4,8,128]{2,1,0:T(8,128)} %param.7) | copy-start | bytes 49156
  66.2 15.7 %all-to-all-start.2 = ((f32[32,1,1024]{2,1,0:T(1,128)}), f32[32,1,1024]{2,1,0:T(1,128)S(1)}, u32[]{:S(2)}, u32[]{:S(2)}) async-start(f32[32,1,1024]{2,1,0:T(1,128)} %reshape.155), calls=%async_computation.2 | async-start | bytes 262144 | tf_op jit(solution)/shard_map/all_to_all | solution.py:43
  73.9 1.9 %copy-start.1 = (f32[64,1,1,384]{0,3,1,2:T(8,128)S(1)}, f32[64,1,1,384]{0,3,1,2:T(8,128)}, u32[]{:S(2)}) copy-start(f32[64,1,1,384]{0,3,1,2:T(8,128)} %copy.47) | copy-start | bytes 294916
where the time goes:
time: 84.7 us; the launch traced here: 84.1 us
  starting transfers between devices  35.6 us (42%)
  other arithmetic  19.3 us (23%)
  local copies, waits for them, and re-layouts  14.1 us (17%)
  waiting for transfers between devices  9.24 us (11%)
  matrix products  4.81 us (6%)
  between operations  0.99 us (1%)
    all_to_all x1, starting transfers between devices, on_device(): lax.all_to_all(traces, 'col', split_axis=1, concat_axis=1, tiled=True)  13 us
    all_to_all x1, waiting for transfers between devices, on_device(): lax.all_to_all(traces, 'col', split_axis=1, concat_axis=1, tiled=True)  8.63 us
    add x3, other arithmetic, three_tap(): return side_weight * (lower + upper) + centre_weight * middle  7.61 us
    ppermute x2, starting transfers between devices, padded_2(): lax.ppermute(lax.slice_in_dim(block, block.shape[dim] - width, None, axis...  6.62 us
    ppermute x2, starting transfers between devices, padded_2(): lax.ppermute(lax.slice_in_dim(block, 0, width, axis=dim), axis, backward)  6.39 us
    all_to_all x1, starting transfers between devices, sent_to_all(): lax.all_to_all(jnp.broadcast_to(x[None], (count, *x.shape)), axis, 0, 0,...  5.45 us
    unnamed x20, local copies, waits for them, and re-layouts  5.44 us
    dot_general x1, matrix products, on_device(): lax.dot_general(boundary_matrix.reshape(2 * (own_rows * lax.axis_size('co...  4.81 us
  transfers between devices with their start and end apart: 7, of which 2 were waited for; matrix products, arithmetic and copies ran while one was open for 33% of the time, Pallas kernels for 0%

commit v1 on v0

--- a/solution.py
+++ b/solution.py
@@ -68,7 +68,10 @@
     )
     flat_field = wave_field.reshape(components, cell_total)
     traces = jnp.take(flat_field, ordered, axis=1).astype(jnp.bfloat16)
-    received = lax.all_to_all(traces, "col", split_axis=1, concat_axis=1, tiled=True)
+    received = jnp.concatenate(
+        lax.all_to_all(jnp.stack(jnp.split(traces, lax.axis_size("col"), axis=1)), "col", 0, 0),
+        axis=1,
+    )
     column_traces = gather_directly(received, "row", 1)
     padded = padded_2(wave_field, (("row", 2), ("col", 1)), 1)
     padded = jnp.pad(padded, ((0, 0), (0, 0), (0, 0), (1, 1)))

time: 84.7 us -> 91.3 us (1.078)
  starting transfers between devices: 35.6 us -> 48.9 us
  waiting for transfers between devices: 9.24 us -> 2.16 us
    all_to_all x1, starting transfers between devices: 4.16 us -> 18.9 us  [sum_at_owner(): tiles = lax.all_to_all(in_blocks(x, dim, count), axis, 0, 0, tiled=True)]
    all_to_all x1, waiting for transfers between devices: 8.63 us -> 2.14 us  [on_device(): lax.all_to_all(jnp.stack(jnp.split(traces, lax.axis_size('col'), axis=1))...]
    ppermute x2, starting transfers between devices: 6.39 us -> 3.44 us  [padded_2(): lax.ppermute(lax.slice_in_dim(block, 0, width, axis=dim), axis, backward)]
    ppermute x2, starting transfers between devices: 6.62 us -> 7.99 us  [padded_2(): lax.ppermute(lax.slice_in_dim(block, block.shape[dim] - width, None, axis...]
    unnamed x20 -> x51, local copies, waits for them, and re-layouts: 5.44 us -> 5.76 us
  transfers between devices with their start and end apart: 7 -> 7, of which waited for: 2 -> 1; matrix products, arithmetic and copies ran while one was open for 33% -> 31% of each run, Pallas kernels for 0% -> 0%
where the time goes in v1:
time: 91.3 us; the launch traced here: 90.7 us
  starting transfers between devices  48.9 us (54%)
  other arithmetic  19.3 us (21%)
  local copies, waits for them, and re-layouts  14.5 us (16%)
  matrix products  4.81 us (5%)
  waiting for transfers between devices  2.16 us (2%)
  between operations  1.07 us (1%)
    all_to_all x1, starting transfers between devices, sum_at_owner(): tiles = lax.all_to_all(in_blocks(x, dim, count), axis, 0, 0, tiled=True)  18.9 us
    all_to_all x1, starting transfers between devices, on_device(): lax.all_to_all(jnp.stack(jnp.split(traces, lax.axis_size('col'), axis=1))...  12.7 us
    ppermute x2, starting transfers between devices, padded_2(): lax.ppermute(lax.slice_in_dim(block, block.shape[dim] - width, None, axis...  7.99 us
    add x3, other arithmetic, three_tap(): return side_weight * (lower + upper) + centre_weight * middle  7.61 us
    all_to_all x1, starting transfers between devices, sent_to_all(): lax.all_to_all(jnp.broadcast_to(x[None], (count, *x.shape)), axis, 0, 0,...  5.86 us
    unnamed x51, local copies, waits for them, and re-layouts  5.76 us
    dot_general x1, matrix products, on_device(): lax.dot_general(boundary_matrix.reshape(2 * (own_rows * lax.axis_size('co...  4.81 us
    scatter-add x1, other arithmetic, on_device(): flat_image.at[:, node_cell.reshape(node_total)]  3.7 us
  transfers between devices with their start and end apart: 7, of which 1 were waited for; matrix products, arithmetic and copies ran while one was open for 31% of the time, Pallas kernels for 0%

profile of v1, /device:TPU:1, one launch (start us, length us, event | category | flops | bytes accessed | tf_op | source)
XLA Modules:
  0.0 90.7 jit_solution(7664783763376845179)
XLA Ops:
  0.6 0.0 copy-start
  0.7 2.1 %fusion.20 = (f32[64,4,1,128]{3,2,1,0:T(1,128)S(1)}, f32[64,4,1,128]{3,2,1,0:T(1,128)S(1)}) fusion(f32[64,4,8,128]{3,2,1,0:T(8,128)} %param.6), kind=kLoop, calls=%fused_computation.119 | loop fusion | bytes 524288 | tf_op jit(solution)/shard_map/slice | solution.py:28
  2.8 1.3 %collective-permute-start.1 = (f32[64,4,1,128]{3,0,2,1:T(8,128)S(1)}, f32[64,4,1,128]{3,0,2,1:T(8,128)S(1)}, u32[]{:S(2)}, u32[]{:S(2)}) collective-permute-start(f32[64,4,1,128]{3,0,2,1:T(8,128)S(1)} %copy.46), channel_id=1, source_target_pairs={{32,0},{64,32},{96,64},{128,96},{160,128},{192,160},{224,192},{33,... | collective-permute-start | bytes 393224 | tf_op jit(solution)/shard_map/ppermute | solution.py:30
  4.1 4.6 %collective-permute-start = (f32[64,4,1,128]{3,0,2,1:T(8,128)S(1)}, f32[64,4,1,128]{3,0,2,1:T(8,128)S(1)}, u32[]{:S(2)}, u32[]{:S(2)}) collective-permute-start(f32[64,4,1,128]{3,0,2,1:T(8,128)S(1)} %copy.45), channel_id=1, source_target_pairs={{0,32},{32,64},{64,96},{96,128},{128,160},{160,192},{192,224},{1,3... | collective-permute-start | bytes 393224 | tf_op jit(solution)/shard_map/ppermute | solution.py:27
  8.7 1.8 %copy.38 = bf16[64,4,8,128]{0,3,2,1:T(8,128)(2,1)S(1)} copy(f32[64,4,8,128]{3,2,1,0:T(8,128)} %param.6) | data formatting | bytes 1572864 | tf_op args[0]
  10.6 0.1 broadcast_in_dim.44
  10.7 0.1 copy.36
  10.8 0.3 select_reduce_fusion
  11.1 0.1 copy.37
  11.1 0.1 reshape.126
  11.3 0.1 reshape.124
  11.4 1.4 %gather_fusion = bf16[384,64]{1,0:T(8,128)(2,1)S(1)} fusion(bf16[64,4096]{0,1:T(8,128)(2,1)S(1)} %bitcast.161, s32[1024]{0:T(1024)S(1)} %pad_clamp_fusion), kind=kCustom, calls=%fused_computation | custom fusion | bytes 99840 | tf_op jit(solution)/shard_map/jit(_take)/gather | solution.py:70
  12.9 0.1 fusion.17
  13.4 0.8 reshape.152
  14.2 12.7 %all-to-all-start = ((bf16[32,2,384]{2,1,0:T(2,128)(2,1)}), bf16[32,2,384]{2,1,0:T(2,128)(2,1)S(1)}, u32[]{:S(2)}, u32[]{:S(2)}) async-start(bf16[32,2,384]{2,1,0:T(2,128)(2,1)} %reshape.152), calls=%async_computation | async-start | bytes 98304 | tf_op jit(solution)/shard_map/all_to_all | solution.py:72
  26.9 0.1 neg.6
  27.0 0.8 copy.47
  27.8 0.0 collective-permute-done.1
  27.8 0.1 copy.33
  28.0 0.0 collective-permute-done
  28.0 0.1 copy.32
  28.1 0.2 pad_maximum_fusion.3
  28.3 2.1 %collective-permute-start.3 = (f32[64,1,10,128]{3,2,1,0:T(8,128)S(1)}, f32[64,1,10,128]{3,2,1,0:T(8,128)S(1)}, u32[]{:S(2)}, u32[]{:S(2)}) collective-permute-start(f32[64,1,10,128]{3,2,1,0:T(8,128)S(1)} %get-tuple-element.16), channel_id=1, source_target_pairs={{1,0},{2,1},{3,2},{4,3},{5,4},{6,5},{7,6},{8,7},{9,8},{10,9},{11,1... | collective-permute-start | bytes 983048 | tf_op jit(solution)/shard_map/ppermute | solution.py:30
  30.5 3.4 %collective-permute-start.2 = (f32[64,1,10,128]{3,2,1,0:T(8,128)S(1)}, f32[64,1,10,128]{3,2,1,0:T(8,128)}, u32[]{:S(2)}, u32[]{:S(2)}) collective-permute-start(f32[64,1,10,128]{3,2,1,0:T(8,128)S(1)} %get-tuple-element.15), channel_id=1, source_target_pairs={{0,1},{1,2},{2,3},{3,4},{4,5},{5,6},{6,7},{7,8},{8,9},{9,10},{10,1... | collective-permute-start | bytes 983048 | tf_op jit(solution)/shard_map/ppermute | solution.py:27
  33.9 0.6 fusion.18
  34.5 2.1 %all-to-all-done = bf16[32,2,384]{2,1,0:T(2,128)(2,1)S(1)} async-done(((bf16[32,2,384]{2,1,0:T(2,128)(2,1)}), bf16[32,2,384]{2,1,0:T(2,128)(2,1)S(1)}, u32[]{:S(2)}, u32[]{:S(2)}) %all-to-all-start) | async-done | bytes 49184 | tf_op jit(solution)/shard_map/all_to_all | solution.py:72
  36.7 0.1 reshape.153
  36.9 0.1 copy.40
  37.0 0.8 broadcast_in_dim.50
  37.8 5.9 %all-to-all-start.1 = ((bf16[8,64,384]{2,1,0:T(8,128)(2,1)}), bf16[8,64,384]{2,1,0:T(8,128)(2,1)S(1)}, u32[]{:S(2)}, u32[]{:S(2)}) async-start(bf16[8,64,384]{2,1,0:T(8,128)(2,1)} %broadcast_in_dim.50), calls=%async_computation.1 | async-start | bytes 786432 | tf_op jit(solution)/shard_map/all_to_all | solution.py:15
  43.6 0.0 collective-permute-done.2
  43.6 1.5 %pad_maximum_fusion = f32[64,6,10,128]{3,2,1,0:T(8,128)S(1)} fusion(f32[64,1,10,128]{3,2,1,0:T(8,128)S(1)} %collective-permute-done.3, f32[64,4,1,128]{3,2,1,0:T(1,128)S(1)} %copy.33, f32[64,4,8,128]{3,2,1,0:T(8,128)S(1)} %copy-done, f32[64,4,1,128]{3,2,1,0:T(1,128)S(1)} %copy.32, f32[64,1,10,128]{3,2,1,0:T(8,128)} %collective-permute-done.2), kind=kLoop, calls=%fused_computation.5 | loop fusion | flops 1966080 | bytes 3932160 | tf_op jit(solution)/shard_map/concatenate | solution.py:31
  45.2 5.0 %multiply_add_fusion.2 = (f32[64,6,10,128]{3,2,1,0:T(8,128)S(1)}, f32[64,6,10,128]{3,2,1,0:T(8,128)S(1)}, f32[64,6,10,128]{3,2,1,0:T(8,128)S(1)}) fusion(f32[64,6,10,128]{3,2,1,0:T(8,128)S(1)} %pad_maximum_fusion), kind=kLoop, calls=%fused_computation.8 | loop fusion | flops 5406720 | bytes 7864320 | tf_op jit(solution)/shard_map/add | solution.py:52
  50.2 1.6 %fusion.1 = f32[64,6,8,128]{3,2,1,0:T(8,128)} fusion(f32[64,6,10,128]{3,2,1,0:T(8,128)S(1)} %get-tuple-element.14), kind=kLoop, calls=%fused_computation.10 | loop fusion | flops 1572864 | bytes 6291456 | tf_op jit(solution)/shard_map/add | solution.py:52
  51.8 1.0 %multiply_add_fusion.3 = (f32[64,6,8,128]{3,2,1,0:T(8,128)S(1)}, f32[64,6,8,128]{3,2,1,0:T(8,128)S(1)}) fusion(f32[64,6,10,128]{3,2,1,0:T(8,128)S(1)} %get-tuple-element.12, f32[64,6,10,128]{3,2,1,0:T(8,128)S(1)} %get-tuple-element.13), kind=kLoop, calls=%fused_computation.19 | loop fusion | flops 4718592 | bytes 12582912 | tf_op jit(solution)/shard_map/add | solution.py:52
  52.8 0.0 copy-start.3
  52.8 4.8 %convolution_bitcast_fusion = f32[1024,64]{0,1:T(8,128)S(1)} fusion(bf16[64,3072]{1,0:T(8,128)(2,1)S(1)} %bitcast.163, bf16[1024,3072]{1,0:T(8,128)(2,1)} %bitcast.160), kind=kOutput, calls=%fused_computation.20 | convolution fusion | flops 402653184 | bytes 6946816 | tf_op jit(solution)/shard_map/dot_general | solution.py:98
  57.7 0.1 copy.42
  57.8 0.8 reshape.154
  58.7 18.9 %all-to-all-start.2 = ((f32[32,1,1024]{2,1,0:T(1,128)}), f32[32,1,1024]{2,1,0:T(1,128)S(1)}, u32[]{:S(2)}, u32[]{:S(2)}) async-start(f32[32,1,1024]{2,1,0:T(1,128)} %reshape.154), calls=%async_computation.2 | async-start | bytes 262144 | tf_op jit(solution)/shard_map/all_to_all | solution.py:43
  77.6 3.5 %fusion.8 = f32[64,4,8,128]{3,2,1,0:T(8,128)} fusion(f32[64,6,8,128]{3,2,1,0:T(8,128)} %fusion.1, f32[64,6,8,128]{3,2,1,0:T(8,128)S(1)} %get-tuple-element.11, f32[64,6,8,128]{3,2,1,0:T(8,128)S(1)} %get-tuple-element.10, f32[4,8,128]{2,1,0:T(8,128)S(1)} %copy-done.3), kind=kLoop, calls=%fused_computation.24 | loop fusion | flops 3932160 | bytes 10502144 | tf_op jit(solution)/shard_map/sub | solution.py:89
  81.1 1.9 %copy.34 = f32[64,4,8,128]{0,3,2,1:T(8,128)S(1)} copy(f32[64,4,8,128]{3,2,1,0:T(8,128)} %fusion.8) | data formatting | bytes 2097152 | tf_op jit(solution)/shard_map/sub | solution.py:89
  83.1 3.7 %scatter_custom_fusion = f32[64,4096]{0,1:T(8,128)S(1)} fusion(f32[64,4096]{0,1:T(8,128)S(1)} %bitcast.158, s32[384]{0:T(512)} %fusion.18, f32[64,1,1,384]{0,3,1,2:T(8,128)S(1)} %copy-done.1), kind=kCustom, calls=%fused_computation.39 | custom fusion | flops 24576 | bytes 1245184 | tf_op jit(solution)/shard_map/scatter-add | solution.py:91
  86.8 1.8 %copy.43 = f32[64,4,8,128]{3,2,1,0:T(8,128)} copy(f32[64,4,8,128]{0,3,2,1:T(8,128)S(1)} %bitcast.159) | data formatting | bytes 2097152
  88.5 0.5 broadcast.86
  89.0 0.9 %reduce.5 = f32[32,1024]{1,0:T(8,128)S(1)} reduce(f32[32,1,1024]{2,1,0:T(1,128)S(1)} %all-to-all-done.2, f32[]{:T(128)} %broadcast.86), dimensions={1}, to_apply=%all_to_all.11.reduce_sub_computation | reduce | bytes 262148 | tf_op jit(solution)/shard_map/all_to_all | solution.py:43
  90.0 0.1 reshape.155
  90.1 0.6 reduce_sum.19
  (57 shorter events, 0.6 us)
Async XLA Ops:
  0.6 27.5 %copy-start = (f32[64,4,8,128]{3,2,1,0:T(8,128)S(1)}, f32[64,4,8,128]{3,2,1,0:T(8,128)}, u32[]{:S(2)}) copy-start(f32[64,4,8,128]{3,2,1,0:T(8,128)} %param.6) | copy-start | bytes 3145732
  0.6 9.9 %copy-start.4 = (s32[1,1,384]{2,1,0:T(1,128)S(1)}, s32[1,1,384]{2,1,0:T(1,128)}, u32[]{:S(2)}) copy-start(s32[1,1,384]{2,1,0:T(1,128)} %param.9) | copy-start | bytes 4612
  0.7 10.1 %copy-start.5 = (s32[1,1,32]{2,1,0:T(1,128)S(1)}, s32[1,1,32]{2,1,0:T(1,128)}, u32[]{:S(2)}) copy-start(s32[1,1,32]{2,1,0:T(1,128)} %param.10) | copy-start | bytes 388
  0.7 26.2 %copy-start.2 = (f32[64,1,1,384]{3,2,1,0:T(1,128)S(1)}, f32[64,1,1,384]{3,2,1,0:T(1,128)}, u32[]{:S(2)}) copy-start(f32[64,1,1,384]{3,2,1,0:T(1,128)} %param.8) | copy-start | bytes 294916
  2.8 25.0 %collective-permute-start.1 = (f32[64,4,1,128]{3,0,2,1:T(8,128)S(1)}, f32[64,4,1,128]{3,0,2,1:T(8,128)S(1)}, u32[]{:S(2)}, u32[]{:S(2)}) collective-permute-start(f32[64,4,1,128]{3,0,2,1:T(8,128)S(1)} %copy.46), channel_id=1, source_target_pairs={{32,0},{64,32},{96,64},{128,96},{160,128},{192,160},{224,192},{33,... | collective-permute-start | bytes 393224 | tf_op jit(solution)/shard_map/ppermute | solution.py:30
  4.1 23.8 %collective-permute-start = (f32[64,4,1,128]{3,0,2,1:T(8,128)S(1)}, f32[64,4,1,128]{3,0,2,1:T(8,128)S(1)}, u32[]{:S(2)}, u32[]{:S(2)}) collective-permute-start(f32[64,4,1,128]{3,0,2,1:T(8,128)S(1)} %copy.45), channel_id=1, source_target_pairs={{0,32},{32,64},{64,96},{96,128},{128,160},{160,192},{192,224},{1,3... | collective-permute-start | bytes 393224 | tf_op jit(solution)/shard_map/ppermute | solution.py:27
  14.2 22.5 %all-to-all-start = ((bf16[32,2,384]{2,1,0:T(2,128)(2,1)}), bf16[32,2,384]{2,1,0:T(2,128)(2,1)S(1)}, u32[]{:S(2)}, u32[]{:S(2)}) async-start(bf16[32,2,384]{2,1,0:T(2,128)(2,1)} %reshape.152), calls=%async_computation | async-start | bytes 98304 | tf_op jit(solution)/shard_map/all_to_all | solution.py:72
  28.3 15.3 %collective-permute-start.3 = (f32[64,1,10,128]{3,2,1,0:T(8,128)S(1)}, f32[64,1,10,128]{3,2,1,0:T(8,128)S(1)}, u32[]{:S(2)}, u32[]{:S(2)}) collective-permute-start(f32[64,1,10,128]{3,2,1,0:T(8,128)S(1)} %get-tuple-element.16), channel_id=1, source_target_pairs={{1,0},{2,1},{3,2},{4,3},{5,4},{6,5},{7,6},{8,7},{9,8},{10,9},{11,1... | collective-permute-start | bytes 983048 | tf_op jit(solution)/shard_map/ppermute | solution.py:30
  30.5 13.1 %collective-permute-start.2 = (f32[64,1,10,128]{3,2,1,0:T(8,128)S(1)}, f32[64,1,10,128]{3,2,1,0:T(8,128)}, u32[]{:S(2)}, u32[]{:S(2)}) collective-permute-start(f32[64,1,10,128]{3,2,1,0:T(8,128)S(1)} %get-tuple-element.15), channel_id=1, source_target_pairs={{0,1},{1,2},{2,3},{3,4},{4,5},{5,6},{6,7},{7,8},{8,9},{9,10},{10,1... | collective-permute-start | bytes 983048 | tf_op jit(solution)/shard_map/ppermute | solution.py:27
  37.8 15.0 %all-to-all-start.1 = ((bf16[8,64,384]{2,1,0:T(8,128)(2,1)}), bf16[8,64,384]{2,1,0:T(8,128)(2,1)S(1)}, u32[]{:S(2)}, u32[]{:S(2)}) async-start(bf16[8,64,384]{2,1,0:T(8,128)(2,1)} %broadcast_in_dim.50), calls=%async_computation.1 | async-start | bytes 786432 | tf_op jit(solution)/shard_map/all_to_all | solution.py:15
  52.8 24.8 %copy-start.3 = (f32[4,8,128]{2,1,0:T(8,128)S(1)}, f32[4,8,128]{2,1,0:T(8,128)}, u32[]{:S(2)}) copy-start(f32[4,8,128]{2,1,0:T(8,128)} %param.7) | copy-start | bytes 49156
  58.7 29.9 %all-to-all-start.2 = ((f32[32,1,1024]{2,1,0:T(1,128)}), f32[32,1,1024]{2,1,0:T(1,128)S(1)}, u32[]{:S(2)}, u32[]{:S(2)}) async-start(f32[32,1,1024]{2,1,0:T(1,128)} %reshape.154), calls=%async_computation.2 | async-start | bytes 262144 | tf_op jit(solution)/shard_map/all_to_all | solution.py:43
  81.1 1.9 %copy-start.1 = (f32[64,1,1,384]{0,3,1,2:T(8,128)S(1)}, f32[64,1,1,384]{0,3,1,2:T(8,128)}, u32[]{:S(2)}) copy-start(f32[64,1,1,384]{0,3,1,2:T(8,128)} %copy.47) | copy-start | bytes 294916
